TPU v7x, 128 devices: a whole 4x4x4 slice. The times are simulated.
128 devices in a mesh: row: 16 (over y_lo, x, core), col: 8 (over y_hi, z).
Axes of the slice: x: 4, y: 4 (y_hi: 2, y_lo: 2; y = y_hi * 2 + y_lo), z: 4, core: 2. Of those that a mesh axis runs over, the one named last changes fastest.
Arguments:
- cholesky_vectors: float32 [256, 512, 512], P(('row', 'col')), as said below
- factor: float32 [512, 2048], P(('row', 'col')), may hold values from -0.25 to 0.25
- core_weights: float32 [256, 2048], P(('row', 'col')), may hold values from -0.375 to 0.375
Outputs:
- core_gradient: float32 [256, 2048], P(('row', 'col'))
- factor_gradient: float32 [512, 2048], P('row', 'col')
Inputs may be any that keep to these rules, and one draw needn't show every extreme that they name: Each cholesky_vectors[P] is symmetric.
All inputs are finite; a program needn't handle non-finite values.
Results may differ from a plain program's by a relative error of at most 0.0001.
Values sent between devices are 32-bit elements; how exact they have to be, the bound alone decides.
A program may use at most 384 MiB of HBM per device.

v0:
```python
import jax
import jax.numpy as jnp
from jax import lax
from jax.sharding import PartitionSpec as P

AXES = ("row", "col")


def on_device(cholesky_vectors, factor, core_weights):
    high = lax.Precision.HIGHEST
    rank = factor.shape[1]
    rows, cols = (lax.axis_size("row"), lax.axis_size("col"))
    r, c = (lax.axis_index("row"), lax.axis_index("col"))
    x = lax.all_gather(factor, AXES, axis=0, tiled=True)
    z = lax.all_gather(core_weights, AXES, axis=0, tiled=True)
    orbitals, width = (x.shape[0], rank // cols)

    def dot(a, b, dims):
        return lax.dot_general(
            a, b, (dims, ((), ())), precision=high, preferred_element_type=jnp.float32
        )

    adjoint = jnp.einsum(
        "pab,bc->pac", cholesky_vectors, x, precision=high, preferred_element_type=jnp.float32
    )
    projection = jnp.sum(x[None] * adjoint, axis=1)
    part = jnp.sum(adjoint * core_weights[:, None, :], axis=0)
    part = part.reshape(rows, orbitals // rows, cols, width).transpose(0, 2, 1, 3)
    part = part.reshape(rows * cols, orbitals // rows, width)
    summed = lax.psum_scatter(part, AXES, scatter_dimension=0, tiled=True)[0]
    x_c = lax.dynamic_slice_in_dim(x, c * width, width, 1)
    z_c = lax.dynamic_slice_in_dim(z, c * width, width, 1)
    gram = dot(x_c, x, ((0,), (0,)))
    core_gram = dot(z_c, z, ((0,), (0,)))
    x_r = lax.dynamic_slice_in_dim(x, r * (orbitals // rows), orbitals // rows, 0)
    z_r = lax.dynamic_slice_in_dim(z, r * (z.shape[0] // rows), z.shape[0] // rows, 0)
    first = dot(x_r, gram * core_gram, ((1,), (1,)))
    weighted = dot(z_r, gram * gram, ((1,), (1,)))
    own = lax.all_to_all(weighted, "col", split_axis=0, concat_axis=1, tiled=True)
    return (own - projection, 4.0 * (first - summed))


def solution(mesh):
    placed = (P(AXES, None, None), P(AXES, None), P(AXES, None))
    return jax.shard_map(
        on_device,
        mesh=mesh,
        in_specs=placed,
        out_specs=(P(AXES, None), P("row", "col")),
        check_vma=False,
    )
```

profile of v0, /device:TPU:0, one launch (start us, length us, event | category | flops | bytes accessed | tf_op | source)
XLA Modules:
  0.0 1287.9 jit_solution(15794297128244354943)
XLA Ops:
  7.2 0.0 all-gather.7.cloned.1.call-start
  7.2 0.7 all-gather.7.cloned.1.call-update
  7.9 0.0 all-gather.5.cloned.1.call-start
  8.0 0.7 all-gather.5.cloned.1.call-update
  8.7 0.0 reduce-scatter.2.cloned.1.call-start
  8.7 307.2 %all-gather.7.cloned.1.call-done = f32[128,4,2048]{2,1,0:T(4,128)} async-done(((f32[1,4,2048]{2,1,0:T(4,128)}), f32[128,4,2048]{2,1,0:T(4,128)}) %all-gather.7.cloned.1.call-update) | async-done | bytes 4194320 | tf_op jit(solution)/shard_map/all_gather | solution.py:14
  315.9 5.3 reshape.20
  321.2 5.3 reshape.21
  326.5 17.0 %multiply_reduce_fusion = (f32[512,2048]{1,0:T(8,128)S(1)}, f32[2,2048]{1,0:T(2,128)S(1)}) fusion(f32[2,2048]{1,0:T(2,128)S(1)} %copy-done.2, f32[512,2048]{1,0:T(8,128)} %reshape.20, f32[2,512,512]{2,1,0:T(8,128)S(1)} %copy-done, f32[512,2048,1]{1,0,2:T(8,128)} %reshape.21), kind=kOutput, calls=%fused_computation | convolution fusion | flops 12892237824 | bytes 14712832 | tf_op jit(solution)/shard_map/pab,bc->pac/dot_general | solution.py:23
  343.6 2.0 copy.10
  345.5 0.4 bitcast_bitcast_fusion
  345.9 3.3 copy.9
  349.2 272.3 %all-gather.5.cloned.1.call-done = f32[128,2,2048]{2,1,0:T(2,128)} async-done(((f32[1,2,2048]{2,1,0:T(2,128)}), f32[128,2,2048]{2,1,0:T(2,128)}) %all-gather.5.cloned.1.call-update) | async-done | bytes 2097168 | tf_op jit(solution)/shard_map/all_gather | solution.py:15
  621.5 3.7 reshape.18
  625.2 5.5 fusion.3
  630.7 1.3 copy-done.1
  632.0 2.6 fusion
  634.6 0.6 all_to_all.14
  635.3 6.7 all-to-all-start
  642.0 5.6 convolution_multiply_fusion
  647.6 2.2 all-to-all-done
  649.7 0.6 sub.6
  650.3 626.9 %reduce-scatter.2.cloned.1.call-done = f32[1,32,256]{2,1,0:T(8,128)} async-done(((f32[128,32,256]{2,1,0:T(8,128)}), f32[1,32,256]{2,1,0:T(8,128)}) %reduce-scatter.2.cloned.1.call-update) | async-done | bytes 32784 | tf_op jit(solution)/shard_map/reduce_scatter | solution.py:30
  1277.3 4.1 fusion.2
  (6 shorter events, 0.0 us)
Async XLA Ops:
  7.2 319.4 %copy-start = (f32[2,512,512]{2,1,0:T(8,128)S(1)}, f32[2,512,512]{2,1,0:T(8,128)}, u32[]{:S(2)}) copy-start(f32[2,512,512]{2,1,0:T(8,128)} %param.3) | copy-start | bytes 6291460
  7.2 308.7 %all-gather.7.cloned.1.call-start = ((), (), s32[]{:S(2)}) async-start(), calls=%async_computation.4 | async-start | bytes 4227072 | tf_op jit(solution)/shard_map/all_gather | solution.py:14
  7.9 613.6 %all-gather.5.cloned.1.call-start = ((), (), s32[]{:S(2)}) async-start(), calls=%async_computation.3 | async-start | bytes 2113536 | tf_op jit(solution)/shard_map/all_gather | solution.py:15
  8.7 1268.6 %reduce-scatter.2.cloned.1.call-start = ((), (), s32[]{:S(2)}) async-start(), calls=%async_computation.2 | async-start | bytes 4227072 | tf_op jit(solution)/shard_map/reduce_scatter | solution.py:30
  321.2 5.3 copy-start.2
  630.7 1.3 copy-start.1
  635.3 14.4 %all-to-all-start = ((f32[8,2,256]{2,1,0:T(2,128)}), f32[8,2,256]{2,1,0:T(2,128)S(1)}, u32[]{:S(2)}, u32[]{:S(2)}) async-start(f32[8,2,256]{2,1,0:T(2,128)} %all_to_all.14), calls=%async_computation | async-start | bytes 32768 | tf_op jit(solution)/shard_map/all_to_all | solution.py:39
Sparse Core Ops, SparseCore 0:
  9.7 306.1 all-gather.6
  317.6 303.8 all-gather.4
  623.9 653.3 reduce-scatter.1
where the time goes:
time: 1290 us
  waiting for transfers between devices  1210 us (94%)
  matrix products  34.8 us (3%)
  local copies, waits for them, and re-layouts  21.9 us (2%)
  between operations  13.8 us (1%)
    reduce_scatter x1, waiting for transfers between devices, on_device(): summed = lax.psum_scatter(part, AXES, scatter_dimension=0, tiled=True)[0]  627 us
    all_gather x1, waiting for transfers between devices, on_device(): x = lax.all_gather(factor, AXES, axis=0, tiled=True)  307 us
    all_gather x1, waiting for transfers between devices, on_device(): z = lax.all_gather(core_weights, AXES, axis=0, tiled=True)  272 us
  transfers between devices with their start and end apart: 4, of which 4 were waited for; matrix products, arithmetic and copies ran while one was open for 4% of the time, Pallas kernels for 0%

commit v1 on v0

--- a/solution.py
+++ b/solution.py
@@ -6,12 +6,19 @@
 AXES = ("row", "col")
 
 
+def exchange_gather(block, mesh_axis, d):
+    peers = lax.axis_size(mesh_axis)
+    pieces = jnp.stack([block for _ in range(peers)])
+    pieces = lax.all_to_all(pieces, mesh_axis, split_axis=0, concat_axis=0)
+    return jnp.concatenate(pieces, axis=d)
+
+
 def on_device(cholesky_vectors, factor, core_weights):
     high = lax.Precision.HIGHEST
     rank = factor.shape[1]
     rows, cols = (lax.axis_size("row"), lax.axis_size("col"))
     r, c = (lax.axis_index("row"), lax.axis_index("col"))
-    x = lax.all_gather(factor, AXES, axis=0, tiled=True)
+    x = exchange_gather(factor, AXES, 0)
     z = lax.all_gather(core_weights, AXES, axis=0, tiled=True)
     orbitals, width = (x.shape[0], rank // cols)
 

time: 1290 us -> 1010 us (0.78)
  waiting for transfers between devices: 1210 us -> 915 us
    all_gather x1 -> x0, waiting for transfers between devices: 307 us -> none  [on_device(): x = lax.all_gather(factor, AXES, axis=0, tiled=True)]
    all_to_all x0 -> x1, waiting for transfers between devices: none -> 51 us  [exchange_gather(): pieces = lax.all_to_all(pieces, mesh_axis, split_axis=0, concat_axis=0)]
    all_gather x1, waiting for transfers between devices: 272 us -> 238 us  [on_device(): z = lax.all_gather(core_weights, AXES, axis=0, tiled=True)]
  transfers between devices with their start and end apart: 4 -> 4, of which waited for: 4 -> 4; matrix products, arithmetic and copies ran while one was open for 4% -> 5% of each run, Pallas kernels for 0% -> 0%
where the time goes in v1:
time: 1010 us
  waiting for transfers between devices  915 us (91%)
  matrix products  34.8 us (3%)
  local copies, waits for them, and re-layouts  25.8 us (3%)
  starting transfers between devices  18.9 us (2%)
  between operations  14.1 us (1%)
    reduce_scatter x1, waiting for transfers between devices, on_device(): summed = lax.psum_scatter(part, AXES, scatter_dimension=0, tiled=True)[0]  623 us
    all_gather x1, waiting for transfers between devices, on_device(): z = lax.all_gather(core_weights, AXES, axis=0, tiled=True)  238 us
    all_to_all x1, waiting for transfers between devices, exchange_gather(): pieces = lax.all_to_all(pieces, mesh_axis, split_axis=0, concat_axis=0)  51 us
  transfers between devices with their start and end apart: 4, of which 4 were waited for; matrix products, arithmetic and copies ran while one was open for 5% of the time, Pallas kernels for 0%

profile of v1, /device:TPU:0, one launch (start us, length us, event | category | flops | bytes accessed | tf_op | source)
XLA Modules:
  0.0 1009.2 jit_solution(10196879692168396115)
XLA Ops:
  7.2 3.9 stack.2
  11.1 11.7 %all-to-all-start = ((f32[128,4,2048]{2,1,0:T(4,128)}), f32[128,4,2048]{2,1,0:T(4,128)}, u32[]{:S(2)}, u32[]{:S(2)}) async-start(f32[128,4,2048]{2,1,0:T(4,128)} %stack.2), calls=%async_computation | async-start | bytes 8388608 | tf_op jit(solution)/shard_map/all_to_all | solution.py:12
  22.8 0.0 all-gather.3.cloned.1.call-start
  22.8 0.7 all-gather.3.cloned.1.call-update
  23.5 0.0 reduce-scatter.2.cloned.1.call-start
  23.6 51.0 %all-to-all-done = f32[128,4,2048]{2,1,0:T(4,128)} async-done(((f32[128,4,2048]{2,1,0:T(4,128)}), f32[128,4,2048]{2,1,0:T(4,128)}, u32[]{:S(2)}, u32[]{:S(2)}) %all-to-all-start) | async-done | bytes 4194336 | tf_op jit(solution)/shard_map/all_to_all | solution.py:12
  74.6 5.3 reshape.20
  79.8 5.3 reshape.25
  85.2 17.0 %multiply_reduce_fusion = (f32[512,2048]{1,0:T(8,128)S(1)}, f32[2,2048]{1,0:T(2,128)S(1)}) fusion(f32[2,2048]{1,0:T(2,128)S(1)} %copy-done.2, f32[512,2048]{1,0:T(8,128)} %reshape.20, f32[2,512,512]{2,1,0:T(8,128)S(1)} %copy-done, f32[512,2048,1]{1,0,2:T(8,128)} %reshape.25), kind=kOutput, calls=%fused_computation | convolution fusion | flops 12892237824 | bytes 14712832 | tf_op jit(solution)/shard_map/pab,bc->pac/dot_general | solution.py:30
  102.2 2.0 copy.10
  104.2 0.4 bitcast_bitcast_fusion
  104.6 3.3 copy.9
  107.9 238.4 %all-gather.3.cloned.1.call-done = f32[128,2,2048]{2,1,0:T(2,128)} async-done(((f32[1,2,2048]{2,1,0:T(2,128)}), f32[128,2,2048]{2,1,0:T(2,128)}) %all-gather.3.cloned.1.call-update) | async-done | bytes 2097168 | tf_op jit(solution)/shard_map/all_gather | solution.py:22
  346.3 3.7 reshape.24
  349.9 5.5 fusion.3
  355.4 1.3 copy-done.1
  356.7 2.6 fusion
  359.4 0.6 all_to_all.18
  360.0 7.1 all-to-all-start.1
  367.2 5.6 convolution_multiply_fusion
  372.7 2.2 all-to-all-done.1
  374.9 0.6 sub.6
  375.5 622.7 %reduce-scatter.2.cloned.1.call-done = f32[1,32,256]{2,1,0:T(8,128)} async-done(((f32[128,32,256]{2,1,0:T(8,128)}), f32[1,32,256]{2,1,0:T(8,128)}) %reduce-scatter.2.cloned.1.call-update) | async-done | bytes 32784 | tf_op jit(solution)/shard_map/reduce_scatter | solution.py:37
  998.2 4.1 fusion.2
  (6 shorter events, 0.0 us)
Async XLA Ops:
  7.2 78.0 %copy-start = (f32[2,512,512]{2,1,0:T(8,128)S(1)}, f32[2,512,512]{2,1,0:T(8,128)}, u32[]{:S(2)}) copy-start(f32[2,512,512]{2,1,0:T(8,128)} %param.3) | copy-start | bytes 6291460
  11.1 63.5 %all-to-all-start = ((f32[128,4,2048]{2,1,0:T(4,128)}), f32[128,4,2048]{2,1,0:T(4,128)}, u32[]{:S(2)}, u32[]{:S(2)}) async-start(f32[128,4,2048]{2,1,0:T(4,128)} %stack.2), calls=%async_computation | async-start | bytes 8388608 | tf_op jit(solution)/shard_map/all_to_all | solution.py:12
  22.8 323.5 %all-gather.3.cloned.1.call-start = ((), (), s32[]{:S(2)}) async-start(), calls=%async_computation.4 | async-start | bytes 2113536 | tf_op jit(solution)/shard_map/all_gather | solution.py:22
  23.5 974.7 %reduce-scatter.2.cloned.1.call-start = ((), (), s32[]{:S(2)}) async-start(), calls=%async_computation.3 | async-start | bytes 4227072 | tf_op jit(solution)/shard_map/reduce_scatter | solution.py:37
  79.8 5.3 copy-start.2
  355.4 1.3 copy-start.1
  360.0 14.9 %all-to-all-start.1 = ((f32[8,2,256]{2,1,0:T(2,128)}), f32[8,2,256]{2,1,0:T(2,128)S(1)}, u32[]{:S(2)}, u32[]{:S(2)}) async-start(f32[8,2,256]{2,1,0:T(2,128)} %all_to_all.18), calls=%async_computation.1 | async-start | bytes 32768 | tf_op jit(solution)/shard_map/all_to_all | solution.py:46
Sparse Core Ops, SparseCore 0:
  25.3 320.9 all-gather.2
  348.6 649.5 reduce-scatter.1
